TPU v7x, 256 devices: a whole 4x4x8 slice. The times are simulated.
256 devices in a mesh: chan: 32 (over z, x_hi, core), row: 4 (over y), col: 2 (over x_lo).
Axes of the slice: x: 4 (x_hi: 2, x_lo: 2; x = x_hi * 2 + x_lo), y: 4, z: 8, core: 2. Of those that a mesh axis runs over, the one named last changes fastest.
Arguments:
- voltages: bfloat16 [1024, 262144], P('chan', ('row', 'col')), may hold values from -6 to 6
Outputs:
- visibilities: float32 [256, 2, 1024, 1024], P('chan', None, 'row', 'col')
All inputs are finite; a program needn't handle non-finite values.
Results may differ from a plain program's by a relative error of at most 0.0053.
Values may be sent and summed in bfloat16 or wider, within the bound.
No kernel may reach another device: no remote copies, remote signals or barrier semaphores. Data moves between devices by JAX's collectives and lax.ppermute only.
A program may use at most 128 MiB of HBM per device.

v0:
```python
import jax
import jax.numpy as jnp
from jax import lax
from jax.sharding import PartitionSpec as P

FFT_LEN = 512
TAPS = 8
CHANNELS = 256


def shifted(value, axis, by):
    length = lax.axis_size(axis)
    pairs = [(i, i + by) for i in range(length) if 0 <= i + by < length]
    return lax.ppermute(value, axis, pairs)


def window_table(taps, length):
    count = taps * length
    position = jnp.arange(count).astype(jnp.float32)
    offset = (position - count / 2 + 0.5) / length
    taper = 0.5 - 0.5 * jnp.cos(2.0 * jnp.pi * (position + 0.5) / count)
    values = jnp.sinc(offset) * taper
    values = values / jnp.sqrt(jnp.sum(values * values))
    return values.reshape(taps, length)


def fourier_table(channels, length):
    channel_index = jnp.arange(channels, dtype=jnp.int32)[:, None]
    sample_index = jnp.arange(length, dtype=jnp.int32)[None, :]
    phase = (channel_index * sample_index % length).astype(jnp.float32) * (2.0 * jnp.pi / length)
    return jnp.stack([jnp.cos(phase), -jnp.sin(phase)], axis=1).astype(jnp.bfloat16)


def per_device(voltages):
    local_inputs = voltages.shape[0]
    slot_spectra = voltages.shape[1] // FFT_LEN
    window = window_table(TAPS, FFT_LEN)
    table = fourier_table(CHANNELS, FFT_LEN)
    tail = voltages[:, (slot_spectra - TAPS + 1) * FFT_LEN :]
    earlier = shifted(tail, ("row", "col"), 1)
    extended = jnp.concatenate([earlier, voltages], axis=1).reshape(
        local_inputs, slot_spectra + TAPS - 1, FFT_LEN
    )
    total = jnp.zeros((local_inputs, slot_spectra, FFT_LEN), jnp.float32)
    for tap_index in range(TAPS):
        total = total + window[tap_index][None, None, :] * extended[
            :, tap_index : tap_index + slot_spectra, :
        ].astype(jnp.float32)
    filtered = total.astype(jnp.bfloat16)
    spectra = jnp.einsum(
        "kpn,isn->kpsi", table, filtered, preferred_element_type=jnp.float32
    ).astype(jnp.bfloat16)
    turned = lax.all_to_all(spectra, "chan", split_axis=0, concat_axis=3, tiled=True)
    inputs_all = turned.shape[3]
    row_count = lax.axis_size("row")
    col_count = lax.axis_size("col")
    row_block = inputs_all // row_count
    col_block = inputs_all // col_count
    spectra_total = slot_spectra * row_count * col_count
    row_start = lax.axis_index("row") * row_block
    col_start = lax.axis_index("col") * col_block
    piece = lax.all_gather(turned, ("row", "col"), axis=2, tiled=True)
    left = lax.dynamic_slice_in_dim(piece, row_start, row_block, 3)
    right = lax.dynamic_slice_in_dim(piece, col_start, col_block, 3)
    flipped = jnp.stack([left[:, 1], -left[:, 0]], axis=1)
    real_part = jnp.einsum("cpsi,cpsj->cij", left, right, preferred_element_type=jnp.float32)
    imag_part = jnp.einsum("cpsi,cpsj->cij", flipped, right, preferred_element_type=jnp.float32)
    summed = jnp.stack([real_part, imag_part], axis=1)
    return summed / spectra_total


def solution(mesh):
    placed = (P("chan", ("row", "col")),)
    return jax.shard_map(
        per_device,
        mesh=mesh,
        in_specs=placed,
        out_specs=P("chan", None, "row", "col"),
        check_vma=False,
    )
```

profile of v0, /device:TPU:1, one launch (start us, length us, event | category | flops | bytes accessed | tf_op | source)
XLA Modules:
  0.0 496.5 jit_solution(200310706514286712)
XLA Ops:
  6.5 0.0 all-gather.2.cloned.1.call-start
  6.5 1.0 slice.66
  7.5 4.0 collective-permute-start
  11.5 0.7 multiply_reduce_fusion
  12.2 2.2 negate_convert_fusion
  15.0 0.1 broadcast_divide_fusion
  15.1 0.6 collective-permute-done
  15.7 1.7 pad_maximum_fusion
  17.4 2.6 reshape.97
  20.1 11.7 %convert_bitcast_fusion = bf16[256,2,64,32]{0,2,1,3:T(8,128)(2,1)S(1)} fusion(bf16[32,71,512]{2,1,0:T(8,128)(2,1)} %reshape.97, f32[512]{0:T(512)S(1)} %get-tuple-element.8, f32[512]{0:T(512)S(1)} %get-tuple-element.9, f32[512]{0:T(512)S(1)} %get-tuple-element.10, f32[512]{0:T(512)S(1)} %get-tuple-element.11, f32[512]{0:T(512)S(1)} %get-tuple-element.12, ...), kind=kOutput, calls=%fused_computation.16 | convolution fusion | flops 1101004800 | bytes 19415040 | tf_op jit(solution)/shard_map/kpn,isn->kpsi/dot_general | solution.py:50
  31.8 7.6 %copy.12 = bf16[256,2,64,32]{2,1,3,0:T(2,128)(2,1)} copy(bf16[256,2,64,32]{0,2,1,3:T(8,128)(2,1)S(1)} %convert_bitcast_fusion) | data formatting | bytes 4194304 | tf_op jit(solution)/shard_map/convert_element_type | solution.py:52
  39.5 9.1 %reshape.102 = bf16[32,2,16384]{2,1,0:T(2,128)(2,1)S(1)} reshape(bf16[256,32,2,64]{3,2,1,0:T(2,128)(2,1)} %bitcast.26) | data formatting | bytes 4194304
  48.6 62.7 %all_to_all.18 = bf16[32,2,16384]{2,1,0:T(2,128)(2,1)} all-to-all(bf16[32,2,16384]{2,1,0:T(2,128)(2,1)S(1)} %reshape.102), channel_id=1, replica_groups=mesh['chan'=32,'row'=4,'col'=2] {'chan'}, dimensions={0} | all-to-all | bytes 4194304 | tf_op jit(solution)/shard_map/all_to_all | solution.py:53
  111.3 9.8 %reshape.103 = bf16[256,32,2,64]{3,2,1,0:T(2,128)(2,1)} reshape(bf16[32,2,16384]{2,1,0:T(2,128)(2,1)} %all_to_all.18) | data formatting | bytes 4194304
  121.1 3.2 copy.13
  124.3 2.9 copy.14
  127.2 4.8 copy.15
  132.0 0.0 all-gather.2.cloned.1.call-update
  132.0 327.7 %all-gather.2.cloned.1.call-done = bf16[8,2,512,1024]{3,2,1,0:T(8,128)(2,1)} async-done(((bf16[8,2,64,1024]{3,2,1,0:T(8,128)(2,1)}), bf16[8,2,512,1024]{3,2,1,0:T(8,128)(2,1)}) %all-gather.2.cloned.1.call-update) | async-done | bytes 16777232 | tf_op jit(solution)/shard_map/all_gather | solution.py:62
  459.7 4.1 constant_dynamic-slice_fusion
  463.8 0.0 copy-start
  463.8 9.4 %fusion.8 = f32[8,1,256,512]{3,2,0,1:T(8,128)} fusion(bf16[8,2,512,1024]{3,2,1,0:T(8,128)(2,1)} %all-gather.2.cloned.1.call-done, s32[]{:T(128)S(6)} %select_n.65, s32[]{:T(128)S(6)} %select_n.64), kind=kOutput, calls=%fused_computation.11 | convolution fusion | flops 2147483648 | bytes 16777224 | tf_op jit(solution)/shard_map/cpsi,cpsj->cij/dot_general | solution.py:66
  473.2 1.6 copy-done
  474.7 6.0 %fusion.13 = f32[8,1,256,512]{3,2,0,1:T(8,128)} fusion(bf16[8,2,512,1024]{3,2,1,0:T(8,128)(2,1)S(1)} %copy-done, s32[]{:T(128)S(6)} %select_n.65, bf16[8,1,512,256]{3,2,1,0:T(8,128)(2,1)} %get-tuple-element.6, bf16[8,1,512,256]{3,2,1,0:T(8,128)(2,1)S(1)} %get-tuple-element.5), kind=kOutput, calls=%fused_computation.12 | convolution fusion | flops 2149580800 | bytes 16777220 | tf_op jit(solution)/shard_map/cpsi,cpsj->cij/dot_general | solution.py:67
  480.7 4.5 maximum_multiply_fusion
  485.2 4.4 copy.18
  (1 shorter events, 0.0 us)
Async XLA Ops:
  6.5 453.2 %all-gather.2.cloned.1.call-start = ((), (), s32[]{:S(2)}) async-start(), calls=%async_computation.1 | async-start | bytes 18874368 | tf_op jit(solution)/shard_map/all_gather | solution.py:62
  7.5 8.2 %collective-permute-start = (bf16[32,3584]{1,0:T(8,128)(2,1)S(1)}, bf16[32,3584]{1,0:T(8,128)(2,1)S(1)}, u32[]{:S(2)}, u32[]{:S(2)}) collective-permute-start(bf16[32,3584]{1,0:T(8,128)(2,1)S(1)} %slice.66), channel_id=1, source_target_pairs={{0,1},{1,2},{2,3},{3,4},{4,5},{5,6},{6,7},{8,9},{9,10},{10,11},{11... | collective-permute-start | bytes 688136 | tf_op jit(solution)/shard_map/ppermute | solution.py:14
  463.8 10.9 %copy-start = (bf16[8,2,512,1024]{3,2,1,0:T(8,128)(2,1)S(1)}, bf16[8,2,512,1024]{3,2,1,0:T(8,128)(2,1)}, u32[]{:S(2)}) copy-start(bf16[8,2,512,1024]{3,2,1,0:T(8,128)(2,1)} %all-gather.2.cloned.1.call-done) | copy-start | bytes 50331652
Sparse Core Ops, SparseCore 0:
  132.1 327.5 all-gather.1
where the time goes:
time: 497 us
  waiting for transfers between devices  328 us (66%)
  blocking collectives  62.7 us (13%)
  local copies, waits for them, and re-layouts  47.1 us (9%)
  matrix products  27.1 us (5%)
  between operations  14.2 us (3%)
  other arithmetic  13.3 us (3%)
    all_gather x1, waiting for transfers between devices, per_device(): piece = lax.all_gather(turned, ('row', 'col'), axis=2, tiled=True)  328 us
    all_to_all x1, blocking collectives, per_device(): lax.all_to_all(spectra, 'chan', split_axis=0, concat_axis=3, tiled=True)  62.7 us
    unnamed x4, local copies, waits for them, and re-layouts  20.5 us
    dot_general x1, matrix products, per_device(): jnp.einsum('kpn,isn->kpsi', table, filtered, preferred_element_type=jnp.f...  11.7 us
    all_to_all x3, local copies, waits for them, and re-layouts, per_device(): lax.all_to_all(spectra, 'chan', split_axis=0, concat_axis=3, tiled=True)  10.9 us
  transfers between devices with their start and end apart: 2, of which 2 were waited for; matrix products, arithmetic and copies ran while one was open for 1% of the time, Pallas kernels for 0%

commit v1 on v0

--- a/solution.py
+++ b/solution.py
@@ -32,6 +32,15 @@
 
 
 def per_device(voltages):
+
+    def build_halves(payload, dev_axis):
+        return jnp.concatenate(
+            lax.all_to_all(
+                jnp.stack(jnp.split(payload, lax.psum(1, dev_axis), axis=0), 0), dev_axis, 0, 0
+            ),
+            axis=3,
+        )
+
     local_inputs = voltages.shape[0]
     slot_spectra = voltages.shape[1] // FFT_LEN
     window = window_table(TAPS, FFT_LEN)
@@ -50,7 +59,7 @@
     spectra = jnp.einsum(
         "kpn,isn->kpsi", table, filtered, preferred_element_type=jnp.float32
     ).astype(jnp.bfloat16)
-    turned = lax.all_to_all(spectra, "chan", split_axis=0, concat_axis=3, tiled=True)
+    turned = build_halves(spectra, "chan")
     inputs_all = turned.shape[3]
     row_count = lax.axis_size("row")
     col_count = lax.axis_size("col")

time: 497 us -> 601 us (1.21)
  local copies, waits for them, and re-layouts: 47.1 us -> 149 us
    another operation x0 -> x35, local copies, waits for them, and re-layouts: none -> 82.4 us  [build_halves(): jnp.stack(jnp.split(payload, lax.psum(1, dev_axis), axis=0), 0)]
    unnamed x4 -> x67, local copies, waits for them, and re-layouts: 20.5 us -> 47.8 us
    all_to_all x3 -> x0, local copies, waits for them, and re-layouts: 10.9 us -> none  [per_device(): lax.all_to_all(spectra, 'chan', split_axis=0, concat_axis=3, tiled=True)]
    reshape x0 -> x3, local copies, waits for them, and re-layouts: none -> 10.9 us  [build_halves(): jnp.concatenate(lax.all_to_all(jnp.stack(jnp.split(payload, lax.psum(1, d...]
    convert_element_type x1 -> x0, local copies, waits for them, and re-layouts: 7.64 us -> none  [per_device(): spectra = jnp.einsum('kpn,isn->kpsi', table, filtered, preferred_element_...]
  transfers between devices with their start and end apart: 2 -> 2, of which waited for: 2 -> 2; matrix products, arithmetic and copies ran while one was open for 1% -> 0% of each run, Pallas kernels for 0% -> 0%
where the time goes in v1:
time: 601 us; the launch traced here: 599 us
  waiting for transfers between devices  328 us (55%)
  local copies, waits for them, and re-layouts  149 us (25%)
  blocking collectives  62.8 us (10%)
  matrix products  27 us (4%)
  between operations  14.3 us (2%)
  other arithmetic  13.3 us (2%)
    all_gather x1, waiting for transfers between devices, per_device(): piece = lax.all_gather(turned, ('row', 'col'), axis=2, tiled=True)  328 us
    another operation x35, local copies, waits for them, and re-layouts, build_halves(): jnp.stack(jnp.split(payload, lax.psum(1, dev_axis), axis=0), 0)  82.4 us
    all_to_all x1, blocking collectives, build_halves(): lax.all_to_all(jnp.stack(jnp.split(payload, lax.psum(1, dev_axis), axis=0...  62.8 us
    unnamed x67, local copies, waits for them, and re-layouts  47.8 us
  transfers between devices with their start and end apart: 2, of which 2 were waited for; matrix products, arithmetic and copies ran while one was open for 0% of the time, Pallas kernels for 0%

profile of v1, /device:TPU:1, one launch (start us, length us, event | category | flops | bytes accessed | tf_op | source)
XLA Modules:
  0.0 598.6 jit_solution(12417597769974413305)
XLA Ops:
  7.5 4.0 collective-permute-start
  17.4 2.6 reshape.103
  20.1 11.6 %convert_bitcast_fusion = bf16[256,2,64,32]{0,2,1,3:T(8,128)(2,1)S(1)} fusion(bf16[32,71,512]{2,1,0:T(8,128)(2,1)} %reshape.103, f32[512]{0:T(512)S(1)} %get-tuple-element.40, f32[512]{0:T(512)S(1)} %get-tuple-element.41, f32[512]{0:T(512)S(1)} %get-tuple-element.42, f32[512]{0:T(512)S(1)} %get-tuple-element.43, f32[512]{0:T(512)S(1)} %get-tuple-element.44, ...), kind=kOutput, calls=%fused_computation.16 | convolution fusion | flops 1101004800 | bytes 19415040 | tf_op jit(solution)/shard_map/kpn,isn->kpsi/dot_general | solution.py:59
  31.7 6.7 %slice_bitcast_fusion.19 = (bf16[1,8,2,64,32]{1,3,2,4,0:T(8,128)(2,1)}, bf16[1,8,2,64,32]{1,3,2,4,0:T(8,128)(2,1)}, bf16[1,8,2,64,32]{1,3,2,4,0:T(8,128)(2,1)}, ...) fusion(bf16[256,2,64,32]{0,2,1,3:T(8,128)(2,1)S(1)} %convert_bi, ...), kind=kLoop, calls=%fused_computation.36 | loop fusion | bytes 1703936 | tf_op jit(solution)/shard_map/stack | solution.py:39
  38.4 8.9 %slice_bitcast_fusion = (bf16[1,8,2,64,32]{1,3,2,4,0:T(8,128)(2,1)}, bf16[1,8,2,64,32]{1,3,2,4,0:T(8,128)(2,1)}, bf16[1,8,2,64,32]{1,3,2,4,0:T(8,128)(2,1)}, bf1...) fusion(bf16[256,2,64,32]{0,2,1,3:T(8,128)(2,1)S(1)} %convert_bi, ...), kind=kLoop, calls=%fused_computation.17 | loop fusion | bytes 2490368 | tf_op jit(solution)/shard_map/stack | solution.py:39
  47.3 2.3 copy.58
  49.6 2.3 copy.57
  56.4 2.3 copy.54
  58.6 2.3 copy.53
  63.1 2.3 copy.51
  65.4 2.3 copy.50
  67.7 2.3 copy.49
  69.9 2.3 copy.48
  72.2 2.3 copy.47
  83.8 2.3 copy.73
  88.4 2.3 copy.71
  90.6 2.3 copy.70
  97.4 2.3 copy.67
  104.2 2.3 copy.64
  106.5 2.3 copy.63
  145.7 6.9 %reshape.110 = bf16[32,2,16384]{2,1,0:T(2,128)(2,1)S(1)} reshape(bf16[32,8,2,32,64]{4,3,2,1,0:T(8,128)(2,1)} %bitcast.91) | data formatting | bytes 4194304
  152.6 62.8 %all_to_all.5 = bf16[32,2,16384]{2,1,0:T(2,128)(2,1)} all-to-all(bf16[32,2,16384]{2,1,0:T(2,128)(2,1)S(1)} %reshape.110), channel_id=1, replica_groups=mesh['chan'=32,'row'=4,'col'=2] {'chan'}, dimensions={0} | all-to-all | bytes 4194304 | tf_op jit(solution)/shard_map/all_to_all | solution.py:38
  215.4 7.9 %reshape.111 = bf16[32,8,2,32,64]{4,3,2,1,0:T(8,128)(2,1)} reshape(bf16[32,2,16384]{2,1,0:T(2,128)(2,1)} %all_to_all.5) | data formatting | bytes 4194304
  223.4 3.2 bitcast_bitcast_fusion
  226.5 2.9 copy.78
  229.4 4.8 copy.79
  234.2 327.5 %all-gather.2.cloned.1.call-done = bf16[8,2,512,1024]{3,2,1,0:T(8,128)(2,1)} async-done(((bf16[8,2,64,1024]{3,2,1,0:T(8,128)(2,1)}), bf16[8,2,512,1024]{3,2,1,0:T(8,128)(2,1)}) %all-gather.2.cloned.1.call-update) | async-done | bytes 16777232 | tf_op jit(solution)/shard_map/all_gather | solution.py:71
  561.8 4.1 constant_dynamic-slice_fusion
  565.9 9.4 %fusion.8 = f32[8,1,256,512]{3,2,0,1:T(8,128)} fusion(bf16[8,2,512,1024]{3,2,1,0:T(8,128)(2,1)} %all-gather.2.cloned.1.call-done, s32[]{:T(128)S(6)} %select_n.65, s32[]{:T(128)S(6)} %select_n.64), kind=kOutput, calls=%fused_computation.11 | convolution fusion | flops 2147483648 | bytes 16777224 | tf_op jit(solution)/shard_map/cpsi,cpsj->cij/dot_general | solution.py:75
  576.8 6.0 %fusion.13 = f32[8,1,256,512]{3,2,0,1:T(8,128)} fusion(bf16[8,2,512,1024]{3,2,1,0:T(8,128)(2,1)S(1)} %copy-done, s32[]{:T(128)S(6)} %select_n.65, bf16[8,1,512,256]{3,2,1,0:T(8,128)(2,1)} %get-tuple-element.6, bf16[8,1,512,256]{3,2,1,0:T(8,128)(2,1)S(1)} %get-tuple-element.5), kind=kOutput, calls=%fused_computation.12 | convolution fusion | flops 2149580800 | bytes 16777220 | tf_op jit(solution)/shard_map/cpsi,cpsj->cij/dot_general | solution.py:76
  582.8 4.5 maximum_multiply_fusion
  587.3 4.4 copy.82
  (92 shorter events, 72.1 us)
Async XLA Ops:
  6.5 555.2 %all-gather.2.cloned.1.call-start = ((), (), s32[]{:S(2)}) async-start(), calls=%async_computation.1 | async-start | bytes 18874368 | tf_op jit(solution)/shard_map/all_gather | solution.py:71
  7.5 8.2 %collective-permute-start = (bf16[32,3584]{1,0:T(8,128)(2,1)S(1)}, bf16[32,3584]{1,0:T(8,128)(2,1)S(1)}, u32[]{:S(2)}, u32[]{:S(2)}) collective-permute-start(bf16[32,3584]{1,0:T(8,128)(2,1)S(1)} %slice.66), channel_id=1, source_target_pairs={{0,1},{1,2},{2,3},{3,4},{4,5},{5,6},{6,7},{8,9},{9,10},{10,11},{11... | collective-permute-start | bytes 688136 | tf_op jit(solution)/shard_map/ppermute | solution.py:14
  112.0 14.8 %copy-start.10 = (bf16[1,8,2,64,32]{3,4,2,1,0:T(8,128)(2,1)S(1)}, bf16[1,8,2,64,32]{3,4,2,1,0:T(8,128)(2,1)}, u32[]{:S(2)}) copy-start(bf16[1,8,2,64,32]{3,4,2,1,0:T(8,128)(2,1)} %copy.55) | copy-start | bytes 196612
  112.0 15.4 %copy-start.8 = (bf16[1,8,2,64,32]{3,4,2,1,0:T(8,128)(2,1)S(1)}, bf16[1,8,2,64,32]{3,4,2,1,0:T(8,128)(2,1)}, u32[]{:S(2)}) copy-start(bf16[1,8,2,64,32]{3,4,2,1,0:T(8,128)(2,1)} %copy.56) | copy-start | bytes 196612
  112.0 16.1 %copy-start.6 = (bf16[1,8,2,64,32]{3,4,2,1,0:T(8,128)(2,1)S(1)}, bf16[1,8,2,64,32]{3,4,2,1,0:T(8,128)(2,1)}, u32[]{:S(2)}) copy-start(bf16[1,8,2,64,32]{3,4,2,1,0:T(8,128)(2,1)} %copy.57) | copy-start | bytes 196612
  112.0 16.7 %copy-start.4 = (bf16[1,8,2,64,32]{3,4,2,1,0:T(8,128)(2,1)S(1)}, bf16[1,8,2,64,32]{3,4,2,1,0:T(8,128)(2,1)}, u32[]{:S(2)}) copy-start(bf16[1,8,2,64,32]{3,4,2,1,0:T(8,128)(2,1)} %copy.58) | copy-start | bytes 196612
  112.0 27.7 %copy-start.9 = (bf16[1,8,2,64,32]{3,4,2,1,0:T(8,128)(2,1)S(1)}, bf16[1,8,2,64,32]{3,4,2,1,0:T(8,128)(2,1)}, u32[]{:S(2)}) copy-start(bf16[1,8,2,64,32]{3,4,2,1,0:T(8,128)(2,1)} %copy.69) | copy-start | bytes 196612
  112.0 28.3 %copy-start.7 = (bf16[1,8,2,64,32]{3,4,2,1,0:T(8,128)(2,1)S(1)}, bf16[1,8,2,64,32]{3,4,2,1,0:T(8,128)(2,1)}, u32[]{:S(2)}) copy-start(bf16[1,8,2,64,32]{3,4,2,1,0:T(8,128)(2,1)} %copy.70) | copy-start | bytes 196612
  112.1 29.0 %copy-start.5 = (bf16[1,8,2,64,32]{3,4,2,1,0:T(8,128)(2,1)S(1)}, bf16[1,8,2,64,32]{3,4,2,1,0:T(8,128)(2,1)}, u32[]{:S(2)}) copy-start(bf16[1,8,2,64,32]{3,4,2,1,0:T(8,128)(2,1)} %copy.71) | copy-start | bytes 196612
  112.1 29.7 %copy-start.3 = (bf16[1,8,2,64,32]{3,4,2,1,0:T(8,128)(2,1)S(1)}, bf16[1,8,2,64,32]{3,4,2,1,0:T(8,128)(2,1)}, u32[]{:S(2)}) copy-start(bf16[1,8,2,64,32]{3,4,2,1,0:T(8,128)(2,1)} %copy.72) | copy-start | bytes 196612
  113.1 22.6 %copy-start.16 = (bf16[1,8,2,64,32]{3,4,2,1,0:T(8,128)(2,1)S(1)}, bf16[1,8,2,64,32]{3,4,2,1,0:T(8,128)(2,1)}, u32[]{:S(2)}) copy-start(bf16[1,8,2,64,32]{3,4,2,1,0:T(8,128)(2,1)} %copy.63) | copy-start | bytes 196612
  113.1 23.2 %copy-start.15 = (bf16[1,8,2,64,32]{3,4,2,1,0:T(8,128)(2,1)S(1)}, bf16[1,8,2,64,32]{3,4,2,1,0:T(8,128)(2,1)}, u32[]{:S(2)}) copy-start(bf16[1,8,2,64,32]{3,4,2,1,0:T(8,128)(2,1)} %copy.64) | copy-start | bytes 196612
  113.1 23.9 %copy-start.14 = (bf16[1,8,2,64,32]{3,4,2,1,0:T(8,128)(2,1)S(1)}, bf16[1,8,2,64,32]{3,4,2,1,0:T(8,128)(2,1)}, u32[]{:S(2)}) copy-start(bf16[1,8,2,64,32]{3,4,2,1,0:T(8,128)(2,1)} %copy.65) | copy-start | bytes 196612
  113.1 24.6 %copy-start.13 = (bf16[1,8,2,64,32]{3,4,2,1,0:T(8,128)(2,1)S(1)}, bf16[1,8,2,64,32]{3,4,2,1,0:T(8,128)(2,1)}, u32[]{:S(2)}) copy-start(bf16[1,8,2,64,32]{3,4,2,1,0:T(8,128)(2,1)} %copy.66) | copy-start | bytes 196612
  113.1 25.2 %copy-start.12 = (bf16[1,8,2,64,32]{3,4,2,1,0:T(8,128)(2,1)S(1)}, bf16[1,8,2,64,32]{3,4,2,1,0:T(8,128)(2,1)}, u32[]{:S(2)}) copy-start(bf16[1,8,2,64,32]{3,4,2,1,0:T(8,128)(2,1)} %copy.67) | copy-start | bytes 196612
  113.2 25.9 %copy-start.11 = (bf16[1,8,2,64,32]{3,4,2,1,0:T(8,128)(2,1)S(1)}, bf16[1,8,2,64,32]{3,4,2,1,0:T(8,128)(2,1)}, u32[]{:S(2)}) copy-start(bf16[1,8,2,64,32]{3,4,2,1,0:T(8,128)(2,1)} %copy.68) | copy-start | bytes 196612
  113.2 29.2 %copy-start.2 = (bf16[1,8,2,64,32]{3,4,2,1,0:T(8,128)(2,1)S(1)}, bf16[1,8,2,64,32]{3,4,2,1,0:T(8,128)(2,1)}, u32[]{:S(2)}) copy-start(bf16[1,8,2,64,32]{3,4,2,1,0:T(8,128)(2,1)} %copy.73) | copy-start | bytes 196612
  113.2 29.9 %copy-start.1 = (bf16[1,8,2,64,32]{3,4,2,1,0:T(8,128)(2,1)S(1)}, bf16[1,8,2,64,32]{3,4,2,1,0:T(8,128)(2,1)}, u32[]{:S(2)}) copy-start(bf16[1,8,2,64,32]{3,4,2,1,0:T(8,128)(2,1)} %copy.74) | copy-start | bytes 196612
  565.9 10.9 %copy-start = (bf16[8,2,512,1024]{3,2,1,0:T(8,128)(2,1)S(1)}, bf16[8,2,512,1024]{3,2,1,0:T(8,128)(2,1)}, u32[]{:S(2)}) copy-start(bf16[8,2,512,1024]{3,2,1,0:T(8,128)(2,1)} %all-gather.2.cloned.1.call-done) | copy-start | bytes 50331652
Sparse Core Ops, SparseCore 0:
  234.4 327.3 all-gather.1
